TPU v7x, 256 devices: a whole 4x4x8 slice. The times are simulated.
256 devices in a mesh: pipe: 8 (over x_lo, y), expert: 32 (over z, x_hi, core).
Axes of the slice: x: 4 (x_hi: 2, x_lo: 2; x = x_hi * 2 + x_lo), y: 4, z: 8, core: 2. Of those that a mesh axis runs over, the one named last changes fastest.
Arguments:
- tokens: bfloat16 [8, 4096, 2048], P('pipe', 'expert'), may hold values from -6 to 6
- routes: int32 [8, 4096, 6], P('pipe', 'expert'), may hold values from 0 to 31, all different within a row; in each aligned block of 128 rows (0 to 127, 128 to 255, ..., all dimensions but the last counted through in order) at most 36 rows name the same one
- norm_gain: float32 [8, 2048], P('pipe'), may hold values from 0.1 to 1.9
- router_weight: bfloat16 [8, 2048, 32], P('pipe'), may hold values from -0.125 to 0.125
- w_gate: bfloat16 [8, 32, 2048, 768], P('pipe', 'expert'), may hold values from -0.125 to 0.125
- w_up: bfloat16 [8, 32, 2048, 768], P('pipe', 'expert'), may hold values from -0.125 to 0.125
- w_down: bfloat16 [8, 32, 768, 2048], P('pipe', 'expert'), may hold values from -0.21875 to 0.21875
Outputs:
- received: bfloat16 [8, 4096, 2048], P('pipe', 'expert')
Inputs may be any that keep to these rules, and one draw needn't show every extreme that they name: Within each aligned block of 128 tokens of a section (the tokens of one device), the 6 routes of a token name different experts and no expert is named by more than 36 routes; some expert is named by exactly 36 routes in some block; every expert is named somewhere.
All inputs are finite; a program needn't handle non-finite values.
Results may differ from a plain program's by a relative error of at most 0.0039.
Values may be sent and summed in bfloat16 or wider, within the bound.
A program may use at most 128 MiB of HBM per device.

v0:
```python
import jax
import jax.numpy as jnp
from jax import lax
from jax.sharding import PartitionSpec as P


def shifted(shard, axis, by):
    devices = lax.axis_size(axis)
    return lax.ppermute(shard, axis, [(i, (i + by) % devices) for i in range(devices)])


def earlier_matrix(count):
    positions = jnp.arange(count, dtype=jnp.int32)
    return (positions[None, :] < positions[:, None]).astype(jnp.bfloat16)


def slot_ranks(route_block, experts):
    flat_routes = route_block.reshape(-1)
    hits = (flat_routes[:, None] == jnp.arange(experts, dtype=jnp.int32)[None, :]).astype(
        jnp.bfloat16
    )
    before = jnp.dot(earlier_matrix(flat_routes.shape[0]), hits, preferred_element_type=jnp.float32)
    ranks = jnp.sum(before * hits.astype(jnp.float32), axis=1).astype(jnp.int32)
    return ranks.reshape(route_block.shape)


def expert_ffn(slot_block, gate_matrix, up_matrix, down_matrix):
    gate_part = jnp.dot(slot_block, gate_matrix, preferred_element_type=jnp.float32)
    up_part = jnp.dot(slot_block, up_matrix, preferred_element_type=jnp.float32)
    hidden = (jax.nn.silu(gate_part) * up_part).astype(jnp.bfloat16)
    return jnp.dot(hidden, down_matrix, preferred_element_type=jnp.float32).astype(jnp.bfloat16)


def local(tokens, routes, norm_gain, router_weight, w_gate, w_up, w_down):
    local_rows = tokens[0]
    route_local = routes[0]
    gate_matrix = w_gate[0, 0]
    up_matrix = w_up[0, 0]
    down_matrix = w_down[0, 0]
    experts = lax.axis_size("expert")
    tok_dev, top_count = route_local.shape
    model_width = local_rows.shape[1]
    capacity = 3 * tok_dev * top_count // (2 * experts)
    wide_rows = local_rows.astype(jnp.float32)
    mean_square = jnp.mean(wide_rows * wide_rows, axis=-1, keepdims=True)
    normed = (wide_rows * lax.rsqrt(mean_square + 1e-06) * norm_gain[0]).astype(jnp.bfloat16)
    score = jax.nn.sigmoid(jnp.dot(normed, router_weight[0], preferred_element_type=jnp.float32))
    expert_ids = jnp.arange(experts, dtype=jnp.int32)
    chosen = route_local[..., None] == expert_ids[None, None, :]
    picked = jnp.sum(jnp.where(chosen, score[:, None, :], 0.0), axis=-1)
    gate_values = (picked / jnp.sum(picked, axis=1, keepdims=True)).astype(jnp.bfloat16)
    ranks = slot_ranks(route_local, experts)
    slots = route_local * capacity + ranks
    slot_hits = slots[..., None] == jnp.arange(experts * capacity, dtype=jnp.int32)[None, None, :]
    weights_map = jnp.sum(
        jnp.where(slot_hits, gate_values.astype(jnp.float32)[..., None], 0.0), axis=1
    ).astype(jnp.bfloat16)
    table = lax.all_gather(route_local, "expert", axis=0, tiled=True)
    gathered = lax.all_gather(normed, "expert", axis=0, tiled=True)
    own_index = lax.axis_index("expert")
    flat_count = tok_dev * top_count
    blocks = table.reshape(experts, flat_count)
    mine = blocks == own_index
    mine_values = mine.astype(jnp.bfloat16)
    own_ranks = jnp.dot(
        mine_values, earlier_matrix(flat_count).T, preferred_element_type=jnp.float32
    ).astype(jnp.int32)
    matches = mine[..., None] & (
        own_ranks[..., None] == jnp.arange(capacity, dtype=jnp.int32)[None, None, :]
    )
    selector = jnp.any(matches.reshape(experts, tok_dev, top_count, capacity), axis=2).astype(
        jnp.bfloat16
    )
    buffer = jnp.einsum(
        "btc,btd->bcd",
        selector,
        gathered.reshape(experts, tok_dev, model_width),
        preferred_element_type=jnp.float32,
    ).astype(jnp.bfloat16)
    owner_out = expert_ffn(buffer.reshape(-1, model_width), gate_matrix, up_matrix, down_matrix)
    returned = lax.all_to_all(
        owner_out.reshape(experts, capacity, model_width),
        "expert",
        split_axis=0,
        concat_axis=0,
        tiled=True,
    )
    moe = jnp.dot(
        weights_map,
        returned.reshape(experts * capacity, model_width),
        preferred_element_type=jnp.float32,
    )
    layer_out = (wide_rows + moe).astype(jnp.bfloat16)[None]
    received = shifted(layer_out, "pipe", 1)
    return received


def solution(mesh):
    return jax.shard_map(
        local,
        mesh=mesh,
        in_specs=(
            P("pipe", "expert", None),
            P("pipe", "expert", None),
            P("pipe", None),
            P("pipe", None, None),
            P("pipe", "expert", None, None),
            P("pipe", "expert", None, None),
            P("pipe", "expert", None, None),
        ),
        out_specs=P("pipe", "expert", None),
        check_vma=False,
    )
```

profile of v0, /device:TPU:2, one launch (start us, length us, event | category | flops | bytes accessed | tf_op | source)
XLA Modules:
  0.0 350.7 jit_solution(5233156969499989968)
XLA Ops:
  6.5 0.0 copy-start
  6.5 0.0 all-gather.3.cloned.1.call-start
  6.5 1.4 fusion.19
  7.9 2.0 fusion.21
  10.0 0.0 all-gather.3.cloned.1.call-update
  10.0 44.4 %all-gather = s32[1,4096,6]{1,0,2:T(1,128)S(1)} all-gather(s32[1,128,6]{1,0,2:T(1,128)} %param.8), channel_id=2, replica_groups=mesh['pipe'=8,'expert'=32] {'expert'}, dimensions={1}, use_global_device_ids=true | all-gather | bytes 101376 | tf_op jit(solution)/shard_map/all_gather | solution.py:58
  54.4 0.9 fusion.35
  55.3 1.5 copy.23
  56.8 2.5 eq.86
  59.3 1.0 fusion.14
  60.3 1.1 copy.24
  61.4 0.8 eq.87
  62.2 1.2 copy.25
  63.4 0.8 copy.33
  64.2 0.5 fusion.1
  64.7 85.4 %all-gather.3.cloned.1.call-done = bf16[4096,2048]{1,0:T(8,128)(2,1)} async-done(((bf16[128,2048]{1,0:T(8,128)(2,1)}), bf16[4096,2048]{1,0:T(8,128)(2,1)}) %all-gather.3.cloned.1.call-update) | async-done | bytes 16777232 | tf_op jit(solution)/shard_map/all_gather | solution.py:59
  150.0 10.4 %convolution_convert_fusion.1 = bf16[32,36,2048]{2,1,0:T(8,128)(2,1)} fusion(bf16[32,128,2048]{2,1,0:T(8,128)(2,1)} %bitcast.55, pred[32,128,36]{1,0,2:T(8,128)(4,1)S(1)} %fusion.1), kind=kOutput, calls=%fused_computation.1 | convolution fusion | flops 606339072 | bytes 21643264 | tf_op jit(solution)/shard_map/btc,btd->bcd/dot_general | solution.py:74
  160.4 7.2 %reshape.90 = bf16[1152,2048]{1,0:T(8,128)(2,1)} reshape(bf16[32,36,2048]{2,1,0:T(8,128)(2,1)} %convolution_convert_fusion.1) | data formatting | bytes 9437184 | tf_op jit(solution)/shard_map/reshape | solution.py:80
  167.7 0.0 copy-start.1
  167.7 0.0 copy-start.4
  167.7 6.8 %fusion.5 = f32[1152,768]{1,0:T(8,128)S(1)} fusion(bf16[1152,2048]{1,0:T(8,128)(2,1)} %reshape.90, bf16[1,1,2048,768]{3,2,1,0:T(8,128)(2,1)} %param.11), kind=kOutput, calls=%fused_computation.11 | convolution fusion | flops 3623878656 | bytes 11403264 | tf_op jit(solution)/shard_map/dot_general | solution.py:28
  174.4 0.0 copy-done.1
  174.4 0.0 copy-done.4
  174.4 4.2 %fusion.2 = bf16[1152,768]{1,0:T(8,128)(2,1)S(1)} fusion(bf16[1152,2048]{1,0:T(8,128)(2,1)S(1)} %copy-done.1, f32[1152,768]{1,0:T(8,128)S(1)} %fusion.5, bf16[1,1,2048,768]{3,2,1,0:T(8,128)(2,1)S(1)} %copy-done.4), kind=kOutput, calls=%fused_computation.8 | convolution fusion | flops 3629187072 | bytes 13172736 | tf_op jit(solution)/shard_map/dot_general | solution.py:29
  178.6 0.0 copy-done
  178.6 5.5 %convolution_convert_fusion = bf16[1152,2048]{1,0:T(8,128)(2,1)} fusion(bf16[1152,768]{1,0:T(8,128)(2,1)S(1)} %fusion.2, bf16[1,1,768,2048]{3,2,1,0:T(8,128)(2,1)S(1)} %copy-done), kind=kOutput, calls=%fused_computation | convolution fusion | flops 3626237952 | bytes 9633792 | tf_op jit(solution)/shard_map/dot_general | solution.py:31
  184.2 7.2 %reshape.91 = bf16[32,36,2048]{2,1,0:T(8,128)(2,1)} reshape(bf16[1152,2048]{1,0:T(8,128)(2,1)} %convolution_convert_fusion) | data formatting | bytes 9437184 | tf_op jit(solution)/shard_map/reshape | solution.py:82
  191.4 0.0 copy-start.2
  191.4 0.0 copy-start.3
  191.4 5.8 %all-to-all-start = ((bf16[32,36,2048]{2,1,0:T(8,128)(2,1)}), bf16[32,36,2048]{2,1,0:T(8,128)(2,1)}, u32[]{:S(2)}, u32[]{:S(2)}) async-start(bf16[32,36,2048]{2,1,0:T(8,128)(2,1)} %reshape.91), calls=%async_computation | async-start | bytes 10485760 | tf_op jit(solution)/shard_map/all_to_all | solution.py:81
  197.2 0.0 copy-done.2
  197.2 0.1 copy.19
  197.3 0.1 eq.73
  197.5 0.4 fusion.15
  197.8 0.1 convert_element_type.75
  198.0 0.1 copy.21
  198.1 0.0 copy-done.3
  198.1 1.5 fusion.18
  199.6 0.5 select_reduce_fusion
  200.1 116.3 %all-to-all-done = bf16[32,36,2048]{2,1,0:T(8,128)(2,1)} async-done(((bf16[32,36,2048]{2,1,0:T(8,128)(2,1)}), bf16[32,36,2048]{2,1,0:T(8,128)(2,1)}, u32[]{:S(2)}, u32[]{:S(2)}) %all-to-all-start) | async-done | bytes 4718624 | tf_op jit(solution)/shard_map/all_to_all | solution.py:81
  316.4 7.2 %reshape.92 = bf16[1152,2048]{1,0:T(8,128)(2,1)} reshape(bf16[32,36,2048]{2,1,0:T(8,128)(2,1)} %all-to-all-done) | data formatting | bytes 9437184 | tf_op jit(solution)/shard_map/reshape | solution.py:90
  323.6 3.3 fusion.10
  326.9 1.6 collective-permute-start
  328.5 14.5 %collective-permute-done = bf16[1,128,2048]{2,1,0:T(8,128)(2,1)S(1)} collective-permute-done((bf16[1,128,2048]{2,1,0:T(8,128)(2,1)S(1)}, bf16[1,128,2048]{2,1,0:T(8,128)(2,1)S(1)}, u32[]{:S(2)}, u32[]{:S(2)}) %collective-permute-start) | collective-permute-done | bytes 524320 | tf_op jit(solution)/shard_map/ppermute | solution.py:9
  343.0 0.8 copy.37
  (6 shorter events, 0.1 us)
Async XLA Ops:
  6.5 172.1 %copy-start = (bf16[1,1,768,2048]{3,2,1,0:T(8,128)(2,1)S(1)}, bf16[1,1,768,2048]{3,2,1,0:T(8,128)(2,1)}, u32[]{:S(2)}) copy-start(bf16[1,1,768,2048]{3,2,1,0:T(8,128)(2,1)} %param.13) | copy-start | bytes 9437188
  6.5 143.5 %all-gather.3.cloned.1.call-start = ((), (), s32[]{:S(2)}) async-start(), calls=%async_computation.1 | async-start | bytes 17301504 | tf_op jit(solution)/shard_map/all_gather | solution.py:59
  167.7 6.8 %copy-start.1 = (bf16[1152,2048]{1,0:T(8,128)(2,1)S(1)}, bf16[1152,2048]{1,0:T(8,128)(2,1)}, u32[]{:S(2)}) copy-start(bf16[1152,2048]{1,0:T(8,128)(2,1)} %reshape.90) | copy-start | bytes 14155780
  167.7 6.8 %copy-start.4 = (bf16[1,1,2048,768]{3,2,1,0:T(8,128)(2,1)S(1)}, bf16[1,1,2048,768]{3,2,1,0:T(8,128)(2,1)}, u32[]{:S(2)}) copy-start(bf16[1,1,2048,768]{3,2,1,0:T(8,128)(2,1)} %param.12) | copy-start | bytes 9437188
  191.4 5.8 %copy-start.2 = (s32[1,128,6]{1,0,2:T(1,128)S(1)}, s32[1,128,6]{1,0,2:T(1,128)}, u32[]{:S(2)}) copy-start(s32[1,128,6]{1,0,2:T(1,128)} %param.8) | copy-start | bytes 9220
  191.4 6.7 %copy-start.3 = (f32[1,2048]{1,0:T(1,128)S(1)}, f32[1,2048]{1,0:T(1,128)}, u32[]{:S(2)}) copy-start(f32[1,2048]{1,0:T(1,128)} %param.9) | copy-start | bytes 24580
  191.4 125.0 %all-to-all-start = ((bf16[32,36,2048]{2,1,0:T(8,128)(2,1)}), bf16[32,36,2048]{2,1,0:T(8,128)(2,1)}, u32[]{:S(2)}, u32[]{:S(2)}) async-start(bf16[32,36,2048]{2,1,0:T(8,128)(2,1)} %reshape.91), calls=%async_computation | async-start | bytes 10485760 | tf_op jit(solution)/shard_map/all_to_all | solution.py:81
  326.9 16.1 %collective-permute-start = (bf16[1,128,2048]{2,1,0:T(8,128)(2,1)S(1)}, bf16[1,128,2048]{2,1,0:T(8,128)(2,1)S(1)}, u32[]{:S(2)}, u32[]{:S(2)}) collective-permute-start(bf16[1,128,2048]{2,1,0:T(8,128)(2,1)S(1)} %fusion.10), channel_id=1, source_target_pairs={{0,32},{32,64},{64,96},{96,128},{128,160},{160,192},{192,224},{224... | collective-permute-start | bytes 1572872 | tf_op jit(solution)/shard_map/ppermute | solution.py:9
Sparse Core Ops, SparseCore 0:
  10.1 139.8 all-gather.2
where the time goes:
time: 352 us; the launch traced here: 351 us
  waiting for transfers between devices  216 us (61%)
  blocking collectives  44.4 us (13%)
  matrix products  32.9 us (9%)
  local copies, waits for them, and re-layouts  30.8 us (9%)
  between operations  13.5 us (4%)
  starting transfers between devices  7.39 us (2%)
  other arithmetic  5.4 us (2%)
    all_to_all x1, waiting for transfers between devices, local(): lax.all_to_all(owner_out.reshape(experts, capacity, model_width), 'expert...  116 us
    all_gather x1, waiting for transfers between devices, local(): gathered = lax.all_gather(normed, 'expert', axis=0, tiled=True)  85.4 us
    all_gather x1, blocking collectives, local(): table = lax.all_gather(route_local, 'expert', axis=0, tiled=True)  44.4 us
    ppermute x1, waiting for transfers between devices, shifted(): lax.ppermute(shard, axis, [(i, (i + by) % devices) for i in range(devices)])  14.5 us
    dot_general x1, matrix products, local(): jnp.einsum('btc,btd->bcd', selector, gathered.reshape(experts, tok_dev, m...  10.4 us
    reshape x1, local copies, waits for them, and re-layouts, local(): buffer.reshape(-1, model_width)  7.24 us
    reshape x1, local copies, waits for them, and re-layouts, local(): returned.reshape(experts * capacity, model_width)  7.22 us
    reshape x1, local copies, waits for them, and re-layouts, local(): owner_out.reshape(experts, capacity, model_width)  7.21 us
  transfers between devices with their start and end apart: 3, of which 3 were waited for; matrix products, arithmetic and copies ran while one was open for 4% of the time, Pallas kernels for 0%

commit v1 on v0

--- a/solution.py
+++ b/solution.py
@@ -56,7 +56,9 @@
         jnp.where(slot_hits, gate_values.astype(jnp.float32)[..., None], 0.0), axis=1
     ).astype(jnp.bfloat16)
     table = lax.all_gather(route_local, "expert", axis=0, tiled=True)
-    gathered = lax.all_gather(normed, "expert", axis=0, tiled=True)
+    gathered = jnp.concatenate(
+        lax.all_to_all(jnp.stack([normed] * lax.axis_size("expert")), "expert", 0, 0), axis=0
+    )
     own_index = lax.axis_index("expert")
     flat_count = tok_dev * top_count
     blocks = table.reshape(experts, flat_count)

time: 352 us -> 623 us (1.77)
  blocking collectives: 44.4 us -> 394 us
  waiting for transfers between devices: 216 us -> 131 us
  between operations: 13.5 us -> 0.19 us
  starting transfers between devices: 7.39 us -> 20.3 us
  local copies, waits for them, and re-layouts: 30.8 us -> 37.3 us
    all_gather x1, blocking collectives: 44.4 us -> 394 us  [local(): table = lax.all_gather(route_local, 'expert', axis=0, tiled=True)]
    all_gather x1 -> x0, waiting for transfers between devices: 85.4 us -> none  [local(): gathered = lax.all_gather(normed, 'expert', axis=0, tiled=True)]
    all_to_all x0 -> x1, starting transfers between devices: none -> 10.7 us  [local(): lax.all_to_all(jnp.stack([normed] * lax.axis_size('expert')), 'expert', 0...]
  transfers between devices with their start and end apart: 3 -> 3, of which waited for: 3 -> 2; matrix products, arithmetic and copies ran while one was open for 4% -> 2% of each run, Pallas kernels for 0% -> 0%
where the time goes in v1:
time: 623 us; the launch traced here: 620 us
  blocking collectives  394 us (63%)
  waiting for transfers between devices  131 us (21%)
  local copies, waits for them, and re-layouts  37.3 us (6%)
  matrix products  32.9 us (5%)
  starting transfers between devices  20.3 us (3%)
    all_gather x1, blocking collectives, local(): table = lax.all_gather(route_local, 'expert', axis=0, tiled=True)  394 us
    all_to_all x1, waiting for transfers between devices, local(): lax.all_to_all(owner_out.reshape(experts, capacity, model_width), 'expert...  116 us
    ppermute x1, waiting for transfers between devices, shifted(): lax.ppermute(shard, axis, [(i, (i + by) % devices) for i in range(devices)])  14.5 us
  transfers between devices with their start and end apart: 3, of which 2 were waited for; matrix products, arithmetic and copies ran while one was open for 2% of the time, Pallas kernels for 0%

profile of v1, /device:TPU:2, one launch (start us, length us, event | category | flops | bytes accessed | tf_op | source)
XLA Modules:
  0.0 620.5 jit_solution(9066624061285226528)
XLA Ops:
  0.0 0.0 copy-start
  0.0 1.4 fusion.18
  1.4 1.2 fusion.22
  2.6 0.0 copy-start.1
  2.6 0.8 copy-done.1
  3.4 5.9 stack.2
  9.4 0.0 copy-start.4
  9.4 10.7 %all-to-all-start = ((bf16[32,128,2048]{2,1,0:T(8,128)(2,1)}), bf16[32,128,2048]{2,1,0:T(8,128)(2,1)}, u32[]{:S(2)}, u32[]{:S(2)}) async-start(bf16[32,128,2048]{2,1,0:T(8,128)(2,1)} %stack.2), calls=%async_computation | async-start | bytes 33554432 | tf_op jit(solution)/shard_map/all_to_all | solution.py:60
  20.1 0.0 copy-done.4
  20.1 394.1 %all-gather = s32[1,4096,6]{1,0,2:T(1,128)S(1)} all-gather(s32[1,128,6]{1,0,2:T(1,128)S(1)} %copy-done.4), channel_id=2, replica_groups=mesh['pipe'=8,'expert'=32] {'expert'}, dimensions={1}, use_global_device_ids=true | all-gather | bytes 101376 | tf_op jit(solution)/shard_map/all_gather | solution.py:58
  414.2 0.3 fusion.29
  414.5 0.6 copy.33
  415.1 1.5 copy.23
  416.6 2.5 eq.86
  419.1 1.0 fusion.13
  420.1 1.1 copy.24
  421.2 0.8 eq.87
  422.0 1.2 copy.25
  423.2 1.2 fusion.1
  424.5 0.0 all-to-all-done
  424.5 10.4 %convolution_convert_fusion.1 = bf16[32,36,2048]{2,1,0:T(8,128)(2,1)} fusion(bf16[32,128,2048]{2,1,0:T(8,128)(2,1)} %all-to-all-done, pred[32,128,36]{1,0,2:T(8,128)(4,1)S(1)} %fusion.1), kind=kOutput, calls=%fused_computation.1 | convolution fusion | flops 606339072 | bytes 21643264 | tf_op jit(solution)/shard_map/btc,btd->bcd/dot_general | solution.py:76
  434.9 7.2 %reshape.100 = bf16[1152,2048]{1,0:T(8,128)(2,1)} reshape(bf16[32,36,2048]{2,1,0:T(8,128)(2,1)} %convolution_convert_fusion.1) | data formatting | bytes 9437184 | tf_op jit(solution)/shard_map/reshape | solution.py:82
  442.1 0.0 copy-start.2
  442.1 0.0 copy-start.5
  442.1 6.8 %fusion.5 = f32[1152,768]{1,0:T(8,128)S(1)} fusion(bf16[1152,2048]{1,0:T(8,128)(2,1)} %reshape.100, bf16[1,1,2048,768]{3,2,1,0:T(8,128)(2,1)} %param.11), kind=kOutput, calls=%fused_computation.11 | convolution fusion | flops 3623878656 | bytes 11403264 | tf_op jit(solution)/shard_map/dot_general | solution.py:28
  448.9 0.0 copy-done.2
  448.9 0.0 copy-done.5
  448.9 4.2 fusion.2
  453.1 0.0 copy-done
  453.1 5.5 convolution_convert_fusion
  458.6 7.2 %reshape.101 = bf16[32,36,2048]{2,1,0:T(8,128)(2,1)} reshape(bf16[1152,2048]{1,0:T(8,128)(2,1)} %convolution_convert_fusion) | data formatting | bytes 9437184 | tf_op jit(solution)/shard_map/reshape | solution.py:84
  465.8 0.0 copy-start.3
  465.8 8.0 %all-to-all-start.1 = ((bf16[32,36,2048]{2,1,0:T(8,128)(2,1)}), bf16[32,36,2048]{2,1,0:T(8,128)(2,1)}, u32[]{:S(2)}, u32[]{:S(2)}) async-start(bf16[32,36,2048]{2,1,0:T(8,128)(2,1)} %reshape.101), calls=%async_computation.1 | async-start | bytes 10485760 | tf_op jit(solution)/shard_map/all_to_all | solution.py:83
  473.8 0.1 copy.19
  473.9 0.1 eq.73
  474.1 0.4 fusion.14
  474.4 0.1 convert_element_type.75
  474.6 0.1 copy.21
  474.6 0.0 copy-done.3
  474.6 1.4 fusion.17
  476.1 0.5 select_reduce_fusion
  476.6 116.4 %all-to-all-done.1 = bf16[32,36,2048]{2,1,0:T(8,128)(2,1)} async-done(((bf16[32,36,2048]{2,1,0:T(8,128)(2,1)}), bf16[32,36,2048]{2,1,0:T(8,128)(2,1)}, u32[]{:S(2)}, u32[]{:S(2)}) %all-to-all-start.1) | async-done | bytes 4718624 | tf_op jit(solution)/shard_map/all_to_all | solution.py:83
  593.0 7.2 %reshape.102 = bf16[1152,2048]{1,0:T(8,128)(2,1)} reshape(bf16[32,36,2048]{2,1,0:T(8,128)(2,1)} %all-to-all-done.1) | data formatting | bytes 9437184 | tf_op jit(solution)/shard_map/reshape | solution.py:92
  600.2 3.3 fusion.10
  603.5 1.7 collective-permute-start
  605.2 14.5 %collective-permute-done = bf16[1,128,2048]{2,1,0:T(8,128)(2,1)S(1)} collective-permute-done((bf16[1,128,2048]{2,1,0:T(8,128)(2,1)S(1)}, bf16[1,128,2048]{2,1,0:T(8,128)(2,1)S(1)}, u32[]{:S(2)}, u32[]{:S(2)}) %collective-permute-start) | collective-permute-done | bytes 524320 | tf_op jit(solution)/shard_map/ppermute | solution.py:9
  619.7 0.8 copy.37
  (6 shorter events, 0.1 us)
Async XLA Ops:
  0.0 453.1 %copy-start = (bf16[1,1,768,2048]{3,2,1,0:T(8,128)(2,1)S(1)}, bf16[1,1,768,2048]{3,2,1,0:T(8,128)(2,1)}, u32[]{:S(2)}) copy-start(bf16[1,1,768,2048]{3,2,1,0:T(8,128)(2,1)} %param.13) | copy-start | bytes 9437188
  2.6 0.8 copy-start.1
  9.4 10.7 %copy-start.4 = (s32[1,128,6]{1,0,2:T(1,128)S(1)}, s32[1,128,6]{1,0,2:T(1,128)}, u32[]{:S(2)}) copy-start(s32[1,128,6]{1,0,2:T(1,128)} %param.8) | copy-start | bytes 9220
  9.4 415.1 %all-to-all-start = ((bf16[32,128,2048]{2,1,0:T(8,128)(2,1)}), bf16[32,128,2048]{2,1,0:T(8,128)(2,1)}, u32[]{:S(2)}, u32[]{:S(2)}) async-start(bf16[32,128,2048]{2,1,0:T(8,128)(2,1)} %stack.2), calls=%async_computation | async-start | bytes 33554432 | tf_op jit(solution)/shard_map/all_to_all | solution.py:60
  442.1 6.8 %copy-start.2 = (bf16[1152,2048]{1,0:T(8,128)(2,1)S(1)}, bf16[1152,2048]{1,0:T(8,128)(2,1)}, u32[]{:S(2)}) copy-start(bf16[1152,2048]{1,0:T(8,128)(2,1)} %reshape.100) | copy-start | bytes 14155780
  442.1 6.8 %copy-start.5 = (bf16[1,1,2048,768]{3,2,1,0:T(8,128)(2,1)S(1)}, bf16[1,1,2048,768]{3,2,1,0:T(8,128)(2,1)}, u32[]{:S(2)}) copy-start(bf16[1,1,2048,768]{3,2,1,0:T(8,128)(2,1)} %param.12) | copy-start | bytes 9437188
  465.8 8.8 %copy-start.3 = (bf16[1,2048,32]{1,2,0:T(8,128)(2,1)S(1)}, bf16[1,2048,32]{1,2,0:T(8,128)(2,1)}, u32[]{:S(2)}) copy-start(bf16[1,2048,32]{1,2,0:T(8,128)(2,1)} %param.10) | copy-start | bytes 393220
  465.8 127.2 %all-to-all-start.1 = ((bf16[32,36,2048]{2,1,0:T(8,128)(2,1)}), bf16[32,36,2048]{2,1,0:T(8,128)(2,1)}, u32[]{:S(2)}, u32[]{:S(2)}) async-start(bf16[32,36,2048]{2,1,0:T(8,128)(2,1)} %reshape.101), calls=%async_computation.1 | async-start | bytes 10485760 | tf_op jit(solution)/shard_map/all_to_all | solution.py:83
  603.5 16.1 %collective-permute-start = (bf16[1,128,2048]{2,1,0:T(8,128)(2,1)S(1)}, bf16[1,128,2048]{2,1,0:T(8,128)(2,1)S(1)}, u32[]{:S(2)}, u32[]{:S(2)}) collective-permute-start(bf16[1,128,2048]{2,1,0:T(8,128)(2,1)S(1)} %fusion.10), channel_id=1, source_target_pairs={{0,32},{32,64},{64,96},{96,128},{128,160},{160,192},{192,224},{224... | collective-permute-start | bytes 1572872 | tf_op jit(solution)/shard_map/ppermute | solution.py:9
